TPU v7x, 32 devices: a whole 2x2x4 slice. The times are simulated.
32 devices in a mesh: row: 2 (over y), col: 16 (over z, x, core).
Axes of the slice: x: 2, y: 2, z: 4, core: 2. Of those that a mesh axis runs over, the one named last changes fastest.
Arguments:
- blocks: float32 [512, 128, 128], P(('row', 'col')), may hold values from -0.3125 to 0.3125
- block_row: int32 [512], P(('row', 'col')), may hold values from 0 to 63, as said below
- block_col: int32 [512], P(('row', 'col')), may hold values from 0 to 63, as said below
- counts: int32 [32], P(('row', 'col')), may hold values from 1 to 16, as said below
- diagonal: float32 [8192], P(('row', 'col')), may hold values from 0.25 to 4
- vector: float32 [8192, 256], P(('row', 'col')), may hold values from -8 to 8
Outputs:
- next_basis: float32 [8192, 256], P(('row', 'col'))
- second_image: float32 [8192, 256], P(('row', 'col'))
- arnoldi_column: float32 [2, 256], replicated
Inputs may be any that keep to these rules, and one draw needn't show every extreme that they name: The slots of device d = r * 16 + c are rows d * 16 to (d + 1) * 16 - 1. Its slot d * 16 + k * 16 + o (k below 1) has block_row // 2 equal to r * 16 + o, and (block_col // 2) % 16 equals c. No pair (block_row, block_col) occurs twice among all slots. `block_col`: paired with block_row as stated there. Only the first counts[d] slots of device d hold blocks; later slots are ignored. Some device has exactly 16.
All inputs are finite; a program needn't handle non-finite values.
Results may differ from a plain program's by a relative error of at most 0.0001.
Values sent between devices are 32-bit elements; how exact they have to be, the bound alone decides.
A program may use at most 64 MiB of HBM per device.

v0:
```python
import math
import jax
import jax.numpy as jnp
from jax import lax
from jax.sharding import PartitionSpec as P


def collect_tiles(products, local_col, live_slot, n_local):
    slot_count = products.shape[0]
    targets = jnp.arange(n_local, dtype=jnp.int32)
    selector = jnp.where(
        (local_col[:, None] == targets[None, :]) & live_slot[:, None], 1.0, 0.0
    ).astype(jnp.float32)
    return jnp.dot(
        selector.T,
        products.reshape(slot_count, -1),
        precision=lax.Precision.HIGHEST,
        preferred_element_type=jnp.float32,
    )


def local_terms(gathered, blocks, local_row, local_col, live_slot, n_local):
    tile_size = blocks.shape[1]
    rhs_count = gathered.shape[1]
    slot_count = blocks.shape[0]
    group_size = math.gcd(slot_count, 32)
    turn_count = slot_count // group_size
    stacked = gathered.reshape(gathered.shape[0] // tile_size, tile_size, rhs_count)

    def advance(turn_id, totals):
        picked = jnp.take(stacked, local_row, axis=0)
        products = jnp.einsum(
            "gab,gak->gbk",
            blocks,
            picked,
            precision=lax.Precision.HIGHEST,
            preferred_element_type=jnp.float32,
        )
        return totals + collect_tiles(products, local_col, live_slot, n_local)

    start_sum = jnp.zeros((n_local, tile_size * rhs_count), jnp.float32)
    return lax.fori_loop(0, turn_count, advance, start_sum)


def per_device(blocks, block_row, block_col, counts, diagonal, vector):
    n_rows = lax.axis_size("row")
    n_cols = lax.axis_size("col")
    tile_size = blocks.shape[1]
    rhs_count = vector.shape[1]
    per_piece = vector.shape[0] // tile_size
    total_rows = vector.shape[0] * n_rows * n_cols
    grid_row = lax.axis_index("row")
    piece_id = block_col // per_piece
    local_col = piece_id // n_cols * per_piece + block_col % per_piece
    live_slot = jnp.arange(blocks.shape[0], dtype=jnp.int32) < counts[0]
    n_local = n_rows * per_piece
    local_row = block_row - grid_row * (n_cols * per_piece)

    def partial_terms(source):
        gathered = lax.all_gather(source, "col", axis=0, tiled=True)
        return local_terms(gathered, blocks, local_row, local_col, live_slot, n_local)

    def apply_transpose(source):
        partial_sums = partial_terms(source).reshape(n_local * tile_size, rhs_count)
        reduced = lax.psum_scatter(partial_sums, "row", scatter_dimension=0, tiled=True)
        return diagonal[:, None] * source + reduced

    squares = lax.psum(jnp.sum(vector * vector, axis=0), ("row", "col"))
    magnitude = jnp.sqrt(squares / total_rows + 1e-06)
    unit_basis = vector / magnitude
    first_image = apply_transpose(unit_basis)
    first_squares, cross_sum, basis_squares = lax.psum(
        (
            jnp.sum(first_image * first_image, axis=0),
            jnp.sum(first_image * unit_basis, axis=0),
            jnp.sum(unit_basis * unit_basis, axis=0),
        ),
        ("row", "col"),
    )
    projection = cross_sum / total_rows
    remainder = first_image - projection * unit_basis
    remainder_power = (
        first_squares - 2.0 * projection * cross_sum + projection * projection * basis_squares
    ) / total_rows
    norm_new = jnp.sqrt(remainder_power + 1e-06)
    next_basis = remainder / norm_new
    second_image = apply_transpose(next_basis)
    return (next_basis, second_image, jnp.stack([projection, norm_new]))


def solution(mesh):
    return jax.shard_map(
        per_device,
        mesh=mesh,
        in_specs=(
            P(("row", "col"), None, None),
            P(("row", "col")),
            P(("row", "col")),
            P(("row", "col")),
            P(("row", "col")),
            P(("row", "col"), None),
        ),
        out_specs=(P(("row", "col"), None), P(("row", "col"), None), P()),
        check_vma=False,
    )
```

profile of v0, /device:TPU:0, one launch (start us, length us, event | category | flops | bytes accessed | tf_op | source)
XLA Modules:
  0.0 259.7 jit_solution(16677184944580297266)
XLA Ops:
  7.2 0.0 copy-start
  7.2 0.0 all-gather.3.cloned.1.call-start
  7.2 1.1 multiply_reduce_fusion.3
  8.3 42.0 %psum.28 = f32[256]{0:T(256)S(1)} all-reduce(f32[256]{0:T(256)S(1)} %multiply_reduce_fusion.3), channel_id=1, replica_groups=mesh['row'=2,'col'=16] {'row','col'}, use_global_device_ids=true, to_apply=%region_1.2 | all-reduce | flops 256 | bytes 2048 | tf_op jit(solution)/shard_map/psum | solution.py:68
  50.3 1.7 broadcast_divide_fusion
  52.0 0.0 all-gather.3.cloned.1.call-update
  52.0 0.0 reduce-scatter.3.cloned.1.call-start
  52.7 0.7 compare_and_fusion
  53.4 0.7 fusion.32
  54.1 48.3 %all-gather.3.cloned.1.call-done = f32[4096,256]{1,0:T(8,128)} async-done(((f32[256,256]{1,0:T(8,128)}), f32[4096,256]{1,0:T(8,128)}) %all-gather.3.cloned.1.call-update) | async-done | bytes 4194320 | tf_op jit(solution)/shard_map/all_gather | solution.py:60
  102.3 2.9 %gather_fusion = f32[16,128,256]{2,1,0:T(8,128)S(1)} fusion(f32[32,128,256]{2,1,0:T(8,128)} %bitcast.24, s32[1024]{0:T(1024)S(1)} %pad_clamp_fusion), kind=kCustom, calls=%fused_computation.clone | custom fusion | bytes 4194368 | tf_op jit(solution)/shard_map/while/body/eval_jaxpr/jit(_take)/gather | solution.py:31
  105.2 0.0 copy-done
  105.2 5.2 %fusion.4 = f32[16,128,256]{1,2,0:T(8,128)} fusion(f32[16,128,128]{2,1,0:T(8,128)S(1)} %copy-done, f32[16,128,256]{2,1,0:T(8,128)S(1)} %gather_fusion, pred[16]{0:T(512)(128)(4,1)S(1)} %get-tuple-element.45), kind=kOutput, calls=%fused_computation.6 | convolution fusion | flops 805830656 | bytes 5242896 | tf_op jit(solution)/shard_map/while/body/eval_jaxpr/gab,gak->gbk/dot_general | solution.py:32
  110.4 2.2 copy.15
  112.6 0.0 copy-start.1
  112.6 0.0 copy-start.3
  112.6 2.0 fusion.16
  114.6 2.2 reshape.42
  116.8 0.0 reduce-scatter.3.cloned.1.call-update
  116.8 0.0 all-gather.5.cloned.1.call-start
  116.9 13.3 %reduce-scatter.3.cloned.1.call-done = f32[256,256]{1,0:T(8,128)} async-done(((f32[512,256]{1,0:T(8,128)}), f32[256,256]{1,0:T(8,128)}) %reduce-scatter.3.cloned.1.call-update) | async-done | bytes 262160 | tf_op jit(solution)/shard_map/reduce_scatter | solution.py:65
  130.1 0.0 copy-done.1
  130.1 0.0 copy-done.3
  130.1 1.1 multiply_reduce_fusion.2
  131.2 39.3 %all-reduce = (f32[256]{0:T(256)S(1)}, f32[256]{0:T(256)S(1)}, f32[256]{0:T(256)S(1)}) all-reduce(f32[256]{0:T(256)S(1)} %get-tuple-element.34, f32[256]{0:T(256)S(1)} %get-tuple-element.33, f32[256]{0:T(256)S(1)} %get-tuple-element.32), channel_id=1, replica_groups=mesh['row'=2,'col'=16] {'row','col'}, use_global_device_ids=true, to_apply=%region_8.10 | all-reduce | flops 768 | bytes 6144 | tf_op jit(solution)/shard_map/psum | solution.py:72
  170.6 1.8 subtract_divide_fusion
  172.3 0.0 all-gather.5.cloned.1.call-update
  172.4 0.2 reduce-scatter.5.cloned.1.call-start
  172.6 51.1 %all-gather.5.cloned.1.call-done = f32[4096,256]{1,0:T(8,128)} async-done(((f32[256,256]{1,0:T(8,128)}), f32[4096,256]{1,0:T(8,128)}) %all-gather.5.cloned.1.call-update) | async-done | bytes 4194320 | tf_op jit(solution)/shard_map/all_gather | solution.py:60
  223.6 2.9 %gather_fusion.1 = f32[16,128,256]{2,1,0:T(8,128)S(1)} fusion(f32[32,128,256]{2,1,0:T(8,128)} %bitcast.25, s32[1024]{0:T(1024)S(1)} %pad_clamp_fusion), kind=kCustom, calls=%fused_computation.1.clone | custom fusion | bytes 4194368 | tf_op jit(solution)/shard_map/while/body/eval_jaxpr/jit(_take)/gather | solution.py:31
  226.5 5.2 %fusion.7 = f32[16,128,256]{1,2,0:T(8,128)} fusion(f32[16,128,128]{2,1,0:T(8,128)S(1)} %copy-done, f32[16,128,256]{2,1,0:T(8,128)S(1)} %gather_fusion.1, pred[16]{0:T(512)(128)(4,1)S(1)} %get-tuple-element.45), kind=kOutput, calls=%fused_computation.7 | convolution fusion | flops 805830656 | bytes 5242896 | tf_op jit(solution)/shard_map/while/body/eval_jaxpr/gab,gak->gbk/dot_general | solution.py:32
  231.7 2.2 copy.16
  233.9 0.0 copy-start.2
  233.9 2.0 fusion.14
  235.9 2.2 reshape.45
  238.1 0.0 reduce-scatter.5.cloned.1.call-update
  238.1 0.6 pad_maximum_fusion
  238.7 12.7 %reduce-scatter.5.cloned.1.call-done = f32[256,256]{1,0:T(8,128)} async-done(((f32[512,256]{1,0:T(8,128)}), f32[256,256]{1,0:T(8,128)}) %reduce-scatter.5.cloned.1.call-update) | async-done | bytes 262160 | tf_op jit(solution)/shard_map/reduce_scatter | solution.py:65
  251.4 0.0 copy-done.2
  251.4 1.8 multiply_add_fusion
  (4 shorter events, 0.0 us)
Async XLA Ops:
  7.2 98.0 %copy-start = (f32[16,128,128]{2,1,0:T(8,128)S(1)}, f32[16,128,128]{2,1,0:T(8,128)}, u32[]{:S(2)}) copy-start(f32[16,128,128]{2,1,0:T(8,128)} %param.8) | copy-start | bytes 3145732
  7.2 95.1 %all-gather.3.cloned.1.call-start = ((), (), s32[]{:S(2)}) async-start(), calls=%async_computation.2 | async-start | bytes 4456448 | tf_op jit(solution)/shard_map/all_gather | solution.py:60
  52.0 78.1 %reduce-scatter.3.cloned.1.call-start = ((), (), s32[]{:S(2)}) async-start(), calls=%async_computation.3 | async-start | bytes 786432 | tf_op jit(solution)/shard_map/reduce_scatter | solution.py:65
  112.6 17.6 %copy-start.1 = (f32[256,256]{1,0:T(8,128)S(1)}, f32[256,256]{1,0:T(8,128)}, u32[]{:S(2)}) copy-start(f32[256,256]{1,0:T(8,128)} %param.13) | copy-start | bytes 786436
  112.6 17.6 %copy-start.3 = (f32[256]{0:T(256)S(1)}, f32[256]{0:T(256)}, u32[]{:S(2)}) copy-start(f32[256]{0:T(256)} %param.12) | copy-start | bytes 3076
  116.8 106.8 %all-gather.5.cloned.1.call-start = ((), (), s32[]{:S(2)}) async-start(), calls=%async_computation.4 | async-start | bytes 4456448 | tf_op jit(solution)/shard_map/all_gather | solution.py:60
  172.4 79.1 %reduce-scatter.5.cloned.1.call-start = ((), (), s32[]{:S(2)}) async-start(), calls=%async_computation.5 | async-start | bytes 786432 | tf_op jit(solution)/shard_map/reduce_scatter | solution.py:65
  233.9 17.5 %copy-start.2 = (f32[256,256]{1,0:T(8,128)S(1)}, f32[256,256]{1,0:T(8,128)}, u32[]{:S(2)}) copy-start(f32[256,256]{1,0:T(8,128)} %subtract_divide_fusion) | copy-start | bytes 786436
Sparse Core Ops, SparseCore 0:
  52.1 50.1 all-gather.2
  116.9 13.1 reduce-scatter.2
  172.5 51.1 all-gather.4
  238.2 13.1 reduce-scatter.4
where the time goes:
time: 260 us
  waiting for transfers between devices  125 us (48%)
  blocking collectives  81.3 us (31%)
  local copies, waits for them, and re-layouts  14.5 us (6%)
  between operations  14.5 us (6%)
  matrix products  14.3 us (6%)
  other arithmetic  9.32 us (4%)
    all_gather x2, waiting for transfers between devices, partial_terms(): gathered = lax.all_gather(source, 'col', axis=0, tiled=True)  99.3 us
    psum x1, blocking collectives, per_device(): squares = lax.psum(jnp.sum(vector * vector, axis=0), ('row', 'col'))  42 us
    psum x1, blocking collectives, per_device(): lax.psum((jnp.sum(first_image * first_image, axis=0), jnp.sum(first_image...  39.3 us
    reduce_scatter x2, waiting for transfers between devices, apply_transpose(): lax.psum_scatter(partial_sums, 'row', scatter_dimension=0, tiled=True)  26 us
    dot_general x2, matrix products, advance(): jnp.einsum('gab,gak->gbk', blocks, picked, precision=lax.Precision.HIGHES...  10.3 us
    gather x2, local copies, waits for them, and re-layouts, advance(): picked = jnp.take(stacked, local_row, axis=0)  5.73 us
  transfers between devices with their start and end apart: 4, of which 4 were waited for; matrix products, arithmetic and copies ran while one was open for 1% of the time, Pallas kernels for 0%

commit v1 on v0

--- a/solution.py
+++ b/solution.py
@@ -65,7 +65,7 @@
         reduced = lax.psum_scatter(partial_sums, "row", scatter_dimension=0, tiled=True)
         return diagonal[:, None] * source + reduced
 
-    squares = lax.psum(jnp.sum(vector * vector, axis=0), ("row", "col"))
+    squares = jnp.sum(lax.all_gather(jnp.sum(vector * vector, axis=0), ("row", "col")), axis=0)
     magnitude = jnp.sqrt(squares / total_rows + 1e-06)
     unit_basis = vector / magnitude
     first_image = apply_transpose(unit_basis)

time: 260 us -> 258 us (level)
  waiting for transfers between devices: 125 us -> 122 us
    all_gather x0 -> x1, blocking collectives: none -> 43.3 us  [per_device(): lax.all_gather(jnp.sum(vector * vector, axis=0), ('row', 'col'))]
    psum x1 -> x0, blocking collectives: 42 us -> none  [per_device(): squares = lax.psum(jnp.sum(vector * vector, axis=0), ('row', 'col'))]
    all_gather x2, waiting for transfers between devices: 99.3 us -> 95.8 us  [partial_terms(): gathered = lax.all_gather(source, 'col', axis=0, tiled=True)]
where the time goes in v1:
time: 258 us
  waiting for transfers between devices  122 us (47%)
  blocking collectives  82.7 us (32%)
  local copies, waits for them, and re-layouts  14.5 us (6%)
  between operations  14.5 us (6%)
  matrix products  14.3 us (6%)
  other arithmetic  9.38 us (4%)
    all_gather x2, waiting for transfers between devices, partial_terms(): gathered = lax.all_gather(source, 'col', axis=0, tiled=True)  95.8 us
    all_gather x1, blocking collectives, per_device(): lax.all_gather(jnp.sum(vector * vector, axis=0), ('row', 'col'))  43.3 us
    psum x1, blocking collectives, per_device(): lax.psum((jnp.sum(first_image * first_image, axis=0), jnp.sum(first_image...  39.3 us
    reduce_scatter x2, waiting for transfers between devices, apply_transpose(): lax.psum_scatter(partial_sums, 'row', scatter_dimension=0, tiled=True)  26 us
    dot_general x2, matrix products, advance(): jnp.einsum('gab,gak->gbk', blocks, picked, precision=lax.Precision.HIGHES...  10.3 us
    gather x2, local copies, waits for them, and re-layouts, advance(): picked = jnp.take(stacked, local_row, axis=0)  5.73 us
  transfers between devices with their start and end apart: 4, of which 4 were waited for; matrix products, arithmetic and copies ran while one was open for 1% of the time, Pallas kernels for 0%

profile of v1, /device:TPU:0, one launch (start us, length us, event | category | flops | bytes accessed | tf_op | source)
XLA Modules:
  0.0 257.6 jit_solution(15492123489450599382)
XLA Ops:
  7.2 0.0 copy-start
  7.2 0.0 all-gather.5.cloned.1.call-start
  7.2 1.1 multiply_reduce_fusion.3
  8.3 43.3 %all-gather.1 = f32[32,1,256]{2,1,0:T(1,128)S(1)} all-gather(f32[1,1,256]{2,1,0:T(1,128)S(1)} %bitcast.29), channel_id=2, replica_groups=mesh['row'=2,'col'=16] {'row','col'}, dimensions={0}, use_global_device_ids=true | all-gather | bytes 33792 | tf_op jit(solution)/shard_map/all_gather | solution.py:68
  51.6 0.1 reduce_sum.46
  51.7 1.7 broadcast_divide_fusion
  53.4 0.0 all-gather.5.cloned.1.call-update
  53.4 0.0 reduce-scatter.3.cloned.1.call-start
  54.1 0.7 compare_and_fusion
  54.8 0.7 fusion.32
  55.5 44.7 %all-gather.5.cloned.1.call-done = f32[4096,256]{1,0:T(8,128)} async-done(((f32[256,256]{1,0:T(8,128)}), f32[4096,256]{1,0:T(8,128)}) %all-gather.5.cloned.1.call-update) | async-done | bytes 4194320 | tf_op jit(solution)/shard_map/all_gather | solution.py:60
  100.2 2.9 %gather_fusion = f32[16,128,256]{2,1,0:T(8,128)S(1)} fusion(f32[32,128,256]{2,1,0:T(8,128)} %bitcast.25, s32[1024]{0:T(1024)S(1)} %pad_clamp_fusion), kind=kCustom, calls=%fused_computation.clone | custom fusion | bytes 4194368 | tf_op jit(solution)/shard_map/while/body/eval_jaxpr/jit(_take)/gather | solution.py:31
  103.1 0.0 copy-done
  103.1 5.2 %fusion.4 = f32[16,128,256]{1,2,0:T(8,128)} fusion(f32[16,128,128]{2,1,0:T(8,128)S(1)} %copy-done, f32[16,128,256]{2,1,0:T(8,128)S(1)} %gather_fusion, pred[16]{0:T(512)(128)(4,1)S(1)} %get-tuple-element.45), kind=kOutput, calls=%fused_computation.6 | convolution fusion | flops 805830656 | bytes 5242896 | tf_op jit(solution)/shard_map/while/body/eval_jaxpr/gab,gak->gbk/dot_general | solution.py:32
  108.3 2.2 copy.19
  110.5 0.0 copy-start.1
  110.5 0.0 copy-start.3
  110.5 2.0 fusion.16
  112.5 2.2 reshape.46
  114.7 0.0 reduce-scatter.3.cloned.1.call-update
  114.7 0.0 all-gather.7.cloned.1.call-start
  114.8 13.3 %reduce-scatter.3.cloned.1.call-done = f32[256,256]{1,0:T(8,128)} async-done(((f32[512,256]{1,0:T(8,128)}), f32[256,256]{1,0:T(8,128)}) %reduce-scatter.3.cloned.1.call-update) | async-done | bytes 262160 | tf_op jit(solution)/shard_map/reduce_scatter | solution.py:65
  128.0 0.0 copy-done.1
  128.0 0.0 copy-done.3
  128.0 1.1 multiply_reduce_fusion.2
  129.1 39.3 %all-reduce = (f32[256]{0:T(256)S(1)}, f32[256]{0:T(256)S(1)}, f32[256]{0:T(256)S(1)}) all-reduce(f32[256]{0:T(256)S(1)} %get-tuple-element.34, f32[256]{0:T(256)S(1)} %get-tuple-element.33, f32[256]{0:T(256)S(1)} %get-tuple-element.32), channel_id=1, replica_groups=mesh['row'=2,'col'=16] {'row','col'}, use_global_device_ids=true, to_apply=%region_8.10 | all-reduce | flops 768 | bytes 6144 | tf_op jit(solution)/shard_map/psum | solution.py:72
  168.5 1.8 subtract_divide_fusion
  170.2 0.0 all-gather.7.cloned.1.call-update
  170.3 0.2 reduce-scatter.5.cloned.1.call-start
  170.5 51.1 %all-gather.7.cloned.1.call-done = f32[4096,256]{1,0:T(8,128)} async-done(((f32[256,256]{1,0:T(8,128)}), f32[4096,256]{1,0:T(8,128)}) %all-gather.7.cloned.1.call-update) | async-done | bytes 4194320 | tf_op jit(solution)/shard_map/all_gather | solution.py:60
  221.5 2.9 %gather_fusion.1 = f32[16,128,256]{2,1,0:T(8,128)S(1)} fusion(f32[32,128,256]{2,1,0:T(8,128)} %bitcast.26, s32[1024]{0:T(1024)S(1)} %pad_clamp_fusion), kind=kCustom, calls=%fused_computation.1.clone | custom fusion | bytes 4194368 | tf_op jit(solution)/shard_map/while/body/eval_jaxpr/jit(_take)/gather | solution.py:31
  224.4 5.2 %fusion.7 = f32[16,128,256]{1,2,0:T(8,128)} fusion(f32[16,128,128]{2,1,0:T(8,128)S(1)} %copy-done, f32[16,128,256]{2,1,0:T(8,128)S(1)} %gather_fusion.1, pred[16]{0:T(512)(128)(4,1)S(1)} %get-tuple-element.45), kind=kOutput, calls=%fused_computation.7 | convolution fusion | flops 805830656 | bytes 5242896 | tf_op jit(solution)/shard_map/while/body/eval_jaxpr/gab,gak->gbk/dot_general | solution.py:32
  229.6 2.2 copy.20
  231.8 0.0 copy-start.2
  231.8 2.0 fusion.14
  233.8 2.2 reshape.49
  236.0 0.0 reduce-scatter.5.cloned.1.call-update
  236.0 0.6 pad_maximum_fusion
  236.6 12.7 %reduce-scatter.5.cloned.1.call-done = f32[256,256]{1,0:T(8,128)} async-done(((f32[512,256]{1,0:T(8,128)}), f32[256,256]{1,0:T(8,128)}) %reduce-scatter.5.cloned.1.call-update) | async-done | bytes 262160 | tf_op jit(solution)/shard_map/reduce_scatter | solution.py:65
  249.3 0.0 copy-done.2
  249.3 1.8 multiply_add_fusion
  (4 shorter events, 0.0 us)
Async XLA Ops:
  7.2 95.9 %copy-start = (f32[16,128,128]{2,1,0:T(8,128)S(1)}, f32[16,128,128]{2,1,0:T(8,128)}, u32[]{:S(2)}) copy-start(f32[16,128,128]{2,1,0:T(8,128)} %param.8) | copy-start | bytes 3145732
  7.2 93.0 %all-gather.5.cloned.1.call-start = ((), (), s32[]{:S(2)}) async-start(), calls=%async_computation.2 | async-start | bytes 4456448 | tf_op jit(solution)/shard_map/all_gather | solution.py:60
  53.4 74.6 %reduce-scatter.3.cloned.1.call-start = ((), (), s32[]{:S(2)}) async-start(), calls=%async_computation.3 | async-start | bytes 786432 | tf_op jit(solution)/shard_map/reduce_scatter | solution.py:65
  110.5 17.6 %copy-start.1 = (f32[256,256]{1,0:T(8,128)S(1)}, f32[256,256]{1,0:T(8,128)}, u32[]{:S(2)}) copy-start(f32[256,256]{1,0:T(8,128)} %param.13) | copy-start | bytes 786436
  110.5 17.6 %copy-start.3 = (f32[256]{0:T(256)S(1)}, f32[256]{0:T(256)}, u32[]{:S(2)}) copy-start(f32[256]{0:T(256)} %param.12) | copy-start | bytes 3076
  114.7 106.8 %all-gather.7.cloned.1.call-start = ((), (), s32[]{:S(2)}) async-start(), calls=%async_computation.4 | async-start | bytes 4456448 | tf_op jit(solution)/shard_map/all_gather | solution.py:60
  170.3 79.1 %reduce-scatter.5.cloned.1.call-start = ((), (), s32[]{:S(2)}) async-start(), calls=%async_computation.5 | async-start | bytes 786432 | tf_op jit(solution)/shard_map/reduce_scatter | solution.py:65
  231.8 17.5 %copy-start.2 = (f32[256,256]{1,0:T(8,128)S(1)}, f32[256,256]{1,0:T(8,128)}, u32[]{:S(2)}) copy-start(f32[256,256]{1,0:T(8,128)} %subtract_divide_fusion) | copy-start | bytes 786436
Sparse Core Ops, SparseCore 0:
  53.5 46.6 all-gather.4
  114.8 13.1 reduce-scatter.2
  170.4 51.1 all-gather.6
  236.1 13.1 reduce-scatter.4
